TPU v7x, 512 devices: a whole 4x4x16 slice. The times are simulated.
512 devices in a mesh: pair: 32 (over y, z_lo), row: 16 (over z_hi, x, core).
Axes of the slice: x: 4, y: 4, z: 16 (z_hi: 2, z_lo: 8; z = z_hi * 8 + z_lo), core: 2. Of those that a mesh axis runs over, the one named last changes fastest.
Arguments:
- factor: float32 [8192, 16384], P('row', 'pair'), may hold values from -6 to 6
- plan: int32 [2, 512], replicated, may hold values from 0 to 511, each once within a row
Outputs:
- rotated: float32 [8192, 16384], P('row', 'pair')
Inputs may be any that keep to these rules, and one draw needn't show every extreme that they name: Each row of plan names every number of 0 to 511 once.
All inputs are finite; a program needn't handle non-finite values.
Results may differ from a plain program's by a relative error of at most 0.0001.
Values sent between devices are 32-bit elements; how exact they have to be, the bound alone decides.
A program may use at most 64 MiB of HBM per device.

v0:
```python
import jax
import jax.numpy as jnp
from jax import lax
from jax.sharding import PartitionSpec as P

BLK = 256
ROUNDS = 2
NS_STEPS = 3


eps_value = 1e-06


def from_behind(value, axis, by):
    devices = lax.axis_size(axis)
    return lax.ppermute(value, axis, [(i, (i + by) % devices) for i in range(devices)])


def product(left, right):
    return jnp.dot(left, right, precision=lax.Precision.HIGHEST, preferred_element_type=jnp.float32)


def sign_table(width, col_ids):
    rows_idx = jnp.arange(width)[:, None]
    cols_idx = col_ids[None, :]
    positive = (rows_idx < BLK) & (cols_idx >= BLK)
    negative = (rows_idx >= BLK) & (cols_idx < BLK)
    sign = jnp.where(positive, 1.0, jnp.where(negative, -1.0, 0.0)).astype(jnp.float32)
    unit = (rows_idx == cols_idx).astype(jnp.float32)
    return (sign, positive, unit)


def shards(factor, plan):
    width = factor.shape[1]
    blocks = factor
    for rnd in range(ROUNDS):
        work = jnp.take(blocks, plan[rnd], axis=1)
        partial_value = product(work.T, work)
        groups = lax.axis_size("row")
        count = width // groups
        half = count // 2
        device = lax.axis_index("row")
        spot = jnp.arange(count)
        own_ids = spot // half * BLK + device * half + spot % half
        mixed = (
            partial_value.reshape(width, 2, groups, half)
            .transpose(0, 2, 1, 3)
            .reshape(width, width)
        )
        columns = lax.psum_scatter(mixed, "row", scatter_dimension=1, tiled=True)
        own_block = jnp.take(columns, own_ids, axis=0)
        own_diag = jnp.diagonal(own_block)
        gathered = lax.all_gather(own_diag, "row", axis=0, tiled=True)
        diag = gathered.reshape(groups, 2, half).transpose(1, 0, 2).reshape(width)
        inverse = 1.0 / jnp.sqrt(diag + eps_value)
        own_inverse = 1.0 / jnp.sqrt(own_diag + eps_value)
        normed = columns * inverse[:, None] * own_inverse[None, :]
        sign, positive, unit = sign_table(width, own_ids)
        local_sq = jnp.sum(jnp.where(positive, normed * normed, 0.0))
        total = lax.psum(local_sq, "row")
        scale = 1.0 / (1.0 + jnp.sqrt(total))
        iterate = unit + sign * normed * scale
        for step in range(NS_STEPS):
            current = iterate
            piece = lax.all_gather(current, "row", axis=1, tiled=True)
            folded = product(piece, product(piece.T, current))
            iterate = 1.5 * current - 0.5 * folded
        turned = product(work, lax.all_gather(iterate, "row", axis=1, tiled=True))
        work = turned.reshape(-1, groups, 2, half).transpose(0, 2, 1, 3).reshape(-1, width)
        second = from_behind(work[:, BLK:], "pair", 1)
        blocks = jnp.concatenate([work[:, :BLK], second], axis=1)
    return blocks


def solution(mesh):
    placed = (P("row", "pair"), P())
    return jax.shard_map(
        shards, mesh=mesh, in_specs=placed, out_specs=P("row", "pair"), check_vma=False
    )
```

profile of v0, /device:TPU:1, one launch (start us, length us, event | category | flops | bytes accessed | tf_op | source)
XLA Modules:
  0.0 1138.3 jit_solution(16740906257814945387)
XLA Ops:
  15.7 109.5 %reduce-scatter.3.cloned.1.call-done = f32[512,32]{0,1:T(8,128)} async-done(((f32[512,512]{0,1:T(8,128)}), f32[512,32]{0,1:T(8,128)}) %reduce-scatter.3.cloned.1.call-update) | async-done | bytes 65552 | tf_op jit(solution)/shard_map/reduce_scatter | solution.py:50
  127.8 63.5 %all-reduce = f32[512]{0:T(512)S(1)} all-reduce(f32[512]{0:T(512)S(1)} %dynamic-update-slice), channel_id=1, replica_groups=mesh['pair'=32,'row'=16] {'row'}, use_global_device_ids=true, to_apply=%add | all-reduce | flops 512 | bytes 4096
  192.3 62.6 %psum.14 = f32[]{:T(128)} all-reduce(f32[]{:T(128)} %fusion.26), channel_id=1, replica_groups=mesh['pair'=32,'row'=16] {'row'}, use_global_device_ids=true, to_apply=%region_2.5 | all-reduce | flops 1 | bytes 8 | tf_op jit(solution)/shard_map/psum | solution.py:60
  256.4 76.3 %all-gather.9.cloned.1.call-done = f32[512,512]{0,1:T(8,128)} async-done(((f32[512,32]{0,1:T(8,128)}), f32[512,512]{0,1:T(8,128)}) %all-gather.9.cloned.1.call-update) | async-done | bytes 1048592 | tf_op jit(solution)/shard_map/all_gather | solution.py:65
  332.7 2.4 fusion.38
  336.6 68.6 %all-gather.11.cloned.1.call-done = f32[512,512]{0,1:T(8,128)} async-done(((f32[512,32]{0,1:T(8,128)}), f32[512,512]{0,1:T(8,128)}) %all-gather.11.cloned.1.call-update) | async-done | bytes 1048592 | tf_op jit(solution)/shard_map/all_gather | solution.py:65
  405.2 2.4 fusion.39
  409.0 68.6 %all-gather.13.cloned.1.call-done = f32[512,512]{0,1:T(8,128)} async-done(((f32[512,32]{0,1:T(8,128)}), f32[512,512]{0,1:T(8,128)}) %all-gather.13.cloned.1.call-update) | async-done | bytes 1048592 | tf_op jit(solution)/shard_map/all_gather | solution.py:65
  477.6 2.4 fusion.40
  481.5 68.6 %all-gather.15.cloned.1.call-done = f32[512,512]{0,1:T(8,128)} async-done(((f32[512,32]{0,1:T(8,128)}), f32[512,512]{0,1:T(8,128)}) %all-gather.15.cloned.1.call-update) | async-done | bytes 1048592 | tf_op jit(solution)/shard_map/all_gather | solution.py:68
  550.1 3.2 fusion.10
  555.6 21.7 %collective-permute-done = f32[512,256]{0,1:T(8,128)S(1)} collective-permute-done((f32[512,256]{0,1:T(8,128)S(1)}, f32[512,256]{0,1:T(8,128)S(1)}, u32[]{:S(2)}, u32[]{:S(2)}) %collective-permute-start) | collective-permute-done | bytes 524320 | tf_op jit(solution)/shard_map/ppermute | solution.py:16
  582.1 95.9 %reduce-scatter.5.cloned.1.call-done = f32[512,32]{0,1:T(8,128)} async-done(((f32[512,512]{0,1:T(8,128)}), f32[512,32]{0,1:T(8,128)}) %reduce-scatter.5.cloned.1.call-update) | async-done | bytes 65552 | tf_op jit(solution)/shard_map/reduce_scatter | solution.py:50
  680.7 63.6 %all-reduce.1 = f32[512]{0:T(512)S(1)} all-reduce(f32[512]{0:T(512)S(1)} %dynamic-update-slice.1), channel_id=1, replica_groups=mesh['pair'=32,'row'=16] {'row'}, use_global_device_ids=true, to_apply=%add.1 | all-reduce | flops 512 | bytes 4096
  745.1 62.6 %psum.15 = f32[]{:T(128)} all-reduce(f32[]{:T(128)} %fusion.27), channel_id=1, replica_groups=mesh['pair'=32,'row'=16] {'row'}, use_global_device_ids=true, to_apply=%region_5.8 | all-reduce | flops 1 | bytes 8 | tf_op jit(solution)/shard_map/psum | solution.py:60
  809.3 76.3 %all-gather.17.cloned.1.call-done = f32[512,512]{0,1:T(8,128)} async-done(((f32[512,32]{0,1:T(8,128)}), f32[512,512]{0,1:T(8,128)}) %all-gather.17.cloned.1.call-update) | async-done | bytes 1048592 | tf_op jit(solution)/shard_map/all_gather | solution.py:65
  885.6 2.4 fusion.41
  889.4 68.6 %all-gather.19.cloned.1.call-done = f32[512,512]{0,1:T(8,128)} async-done(((f32[512,32]{0,1:T(8,128)}), f32[512,512]{0,1:T(8,128)}) %all-gather.19.cloned.1.call-update) | async-done | bytes 1048592 | tf_op jit(solution)/shard_map/all_gather | solution.py:65
  958.0 2.4 fusion.42
  961.8 68.6 %all-gather.21.cloned.1.call-done = f32[512,512]{0,1:T(8,128)} async-done(((f32[512,32]{0,1:T(8,128)}), f32[512,512]{0,1:T(8,128)}) %all-gather.21.cloned.1.call-update) | async-done | bytes 1048592 | tf_op jit(solution)/shard_map/all_gather | solution.py:65
  1030.5 2.4 fusion.43
  1034.2 68.7 %all-gather.23.cloned.1.call-done = f32[512,512]{0,1:T(8,128)} async-done(((f32[512,32]{0,1:T(8,128)}), f32[512,512]{0,1:T(8,128)}) %all-gather.23.cloned.1.call-update) | async-done | bytes 1048592 | tf_op jit(solution)/shard_map/all_gather | solution.py:68
  1102.9 3.2 fusion.6
  1108.2 21.9 %collective-permute-done.1 = f32[512,256]{0,1:T(8,128)S(1)} collective-permute-done((f32[512,256]{0,1:T(8,128)S(1)}, f32[512,256]{0,1:T(8,128)S(1)}, u32[]{:S(2)}, u32[]{:S(2)}) %collective-permute-start.1) | collective-permute-done | bytes 524320 | tf_op jit(solution)/shard_map/ppermute | solution.py:16
  (111 shorter events, 36.0 us)
Async XLA Ops:
  6.5 118.7 %reduce-scatter.3.cloned.1.call-start = ((), (), s32[]{:S(2)}) async-start(), calls=%async_computation.2 | async-start | bytes 1114112 | tf_op jit(solution)/shard_map/reduce_scatter | solution.py:50
  13.6 319.1 %all-gather.9.cloned.1.call-start = ((), (), s32[]{:S(2)}) async-start(), calls=%async_computation.3 | async-start | bytes 1114112 | tf_op jit(solution)/shard_map/all_gather | solution.py:65
  127.6 64.0 %copy-start.12 = (f32[512,32]{0,1:T(8,128)S(1)}, f32[512,32]{0,1:T(8,128)}, u32[]{:S(2)}) copy-start(f32[512,32]{0,1:T(8,128)} %reduce-scatter.3.cloned.1.call-done) | copy-start | bytes 196612
  256.3 76.4 %copy-start.11 = (f32[512,32]{0,1:T(8,128)S(1)}, f32[512,32]{0,1:T(8,128)}, u32[]{:S(2)}) copy-start(f32[512,32]{0,1:T(8,128)} %convert_add_fusion.1) | copy-start | bytes 196612
  256.4 148.8 %all-gather.11.cloned.1.call-start = ((), (), s32[]{:S(2)}) async-start(), calls=%async_computation.4 | async-start | bytes 1114112 | tf_op jit(solution)/shard_map/all_gather | solution.py:65
  336.5 68.7 %copy-start.6 = (f32[512,32]{0,1:T(8,128)S(1)}, f32[512,32]{0,1:T(8,128)}, u32[]{:S(2)}) copy-start(f32[512,32]{0,1:T(8,128)} %fusion.5) | copy-start | bytes 196612
  336.5 141.1 %all-gather.13.cloned.1.call-start = ((), (), s32[]{:S(2)}) async-start(), calls=%async_computation.5 | async-start | bytes 1114112 | tf_op jit(solution)/shard_map/all_gather | solution.py:65
  405.2 2.4 copy-start.1
  408.9 68.7 %copy-start.7 = (f32[512,32]{0,1:T(8,128)S(1)}, f32[512,32]{0,1:T(8,128)}, u32[]{:S(2)}) copy-start(f32[512,32]{0,1:T(8,128)} %fusion.4) | copy-start | bytes 196612
  409.0 141.1 %all-gather.15.cloned.1.call-start = ((), (), s32[]{:S(2)}) async-start(), calls=%async_computation.6 | async-start | bytes 1114112 | tf_op jit(solution)/shard_map/all_gather | solution.py:68
  477.6 2.4 copy-start.2
  481.4 196.7 %reduce-scatter.5.cloned.1.call-start = ((), (), s32[]{:S(2)}) async-start(), calls=%async_computation.7 | async-start | bytes 1114112 | tf_op jit(solution)/shard_map/reduce_scatter | solution.py:50
  553.5 23.8 %collective-permute-start = (f32[512,256]{0,1:T(8,128)S(1)}, f32[512,256]{0,1:T(8,128)S(1)}, u32[]{:S(2)}, u32[]{:S(2)}) collective-permute-start(f32[512,256]{0,1:T(8,128)S(1)} %get-tuple-element.10), channel_id=1, source_target_pairs={{0,16},{16,32},{32,48},{48,64},{64,80},{80,96},{96,112},{112,128},... | collective-permute-start | bytes 1572872 | tf_op jit(solution)/shard_map/ppermute | solution.py:16
  582.1 303.4 %all-gather.17.cloned.1.call-start = ((), (), s32[]{:S(2)}) async-start(), calls=%async_computation.8 | async-start | bytes 1114112 | tf_op jit(solution)/shard_map/all_gather | solution.py:65
  680.4 64.0 %copy-start.13 = (f32[512,32]{0,1:T(8,128)S(1)}, f32[512,32]{0,1:T(8,128)}, u32[]{:S(2)}) copy-start(f32[512,32]{0,1:T(8,128)} %reduce-scatter.5.cloned.1.call-done) | copy-start | bytes 196612
  809.2 76.4 %copy-start.10 = (f32[512,32]{0,1:T(8,128)S(1)}, f32[512,32]{0,1:T(8,128)}, u32[]{:S(2)}) copy-start(f32[512,32]{0,1:T(8,128)} %convert_add_fusion) | copy-start | bytes 196612
  809.2 148.8 %all-gather.19.cloned.1.call-start = ((), (), s32[]{:S(2)}) async-start(), calls=%async_computation.9 | async-start | bytes 1114112 | tf_op jit(solution)/shard_map/all_gather | solution.py:65
  885.6 2.4 copy-start.3
  889.3 68.7 %copy-start.8 = (f32[512,32]{0,1:T(8,128)S(1)}, f32[512,32]{0,1:T(8,128)}, u32[]{:S(2)}) copy-start(f32[512,32]{0,1:T(8,128)} %fusion.2) | copy-start | bytes 196612
  889.3 141.1 %all-gather.21.cloned.1.call-start = ((), (), s32[]{:S(2)}) async-start(), calls=%async_computation.10 | async-start | bytes 1114112 | tf_op jit(solution)/shard_map/all_gather | solution.py:65
  961.8 68.7 %copy-start.9 = (f32[512,32]{0,1:T(8,128)S(1)}, f32[512,32]{0,1:T(8,128)}, u32[]{:S(2)}) copy-start(f32[512,32]{0,1:T(8,128)} %fusion.1) | copy-start | bytes 196612
  961.8 141.1 %all-gather.23.cloned.1.call-start = ((), (), s32[]{:S(2)}) async-start(), calls=%async_computation.11 | async-start | bytes 1114112 | tf_op jit(solution)/shard_map/all_gather | solution.py:68
  1030.5 2.4 copy-start.5
  1106.3 23.8 %collective-permute-start.1 = (f32[512,256]{0,1:T(8,128)S(1)}, f32[512,256]{0,1:T(8,128)S(1)}, u32[]{:S(2)}, u32[]{:S(2)}) collective-permute-start(f32[512,256]{0,1:T(8,128)S(1)} %get-tuple-element.8), channel_id=1, source_target_pairs={{0,16},{16,32},{32,48},{48,64},{64,80},{80,96},{96,112},{112,128},... | collective-permute-start | bytes 1572872 | tf_op jit(solution)/shard_map/ppermute | solution.py:16
  (2 other events, 4.8 us)
Sparse Core Ops, SparseCore 0:
  13.8 111.4 reduce-scatter.2
  256.5 76.1 all-gather.8
  336.6 68.5 all-gather.10
  409.1 68.4 all-gather.12
  481.5 68.4 all-gather.14
  582.2 95.7 reduce-scatter.4
  809.3 76.1 all-gather.16
  889.5 68.4 all-gather.18
  961.9 68.5 all-gather.20
  1034.3 68.4 all-gather.22
where the time goes:
time: 1140 us
  waiting for transfers between devices  813 us (71%)
  blocking collectives  252 us (22%)
  matrix products  32.9 us (3%)
  local copies, waits for them, and re-layouts  16 us (1%)
  between operations  16 us (1%)
    all_gather x6, waiting for transfers between devices, shards(): piece = lax.all_gather(current, 'row', axis=1, tiled=True)  427 us
    reduce_scatter x2, waiting for transfers between devices, shards(): columns = lax.psum_scatter(mixed, 'row', scatter_dimension=1, tiled=True)  205 us
    all_gather x2, waiting for transfers between devices, shards(): turned = product(work, lax.all_gather(iterate, 'row', axis=1, tiled=True))  137 us
    unnamed x2, blocking collectives  127 us
    psum x2, blocking collectives, shards(): total = lax.psum(local_sq, 'row')  125 us
    ppermute x2, waiting for transfers between devices, from_behind(): lax.ppermute(value, axis, [(i, (i + by) % devices) for i in range(devices)])  43.5 us
    dot_general x16, matrix products, product(): jnp.dot(left, right, precision=lax.Precision.HIGHEST, preferred_element_t...  32.9 us
  transfers between devices with their start and end apart: 12, of which 12 were waited for; matrix products, arithmetic and copies ran while one was open for 0% of the time, Pallas kernels for 0%

commit v1 on v0

v1 whole, which is shorter than its diff:
```python
import functools

import jax
import jax.numpy as jnp
from jax import lax
from jax.experimental import pallas as pl
from jax.experimental.pallas import tpu as pltpu
from jax.sharding import PartitionSpec as P

BLK = 256
ROUNDS = 2
WIDTH = 2 * BLK
LANES = 128
XCHIPS = 4
PIECES = 8
PIECE = BLK // PIECES
TALL = 2 * PIECE
PACKED = TALL + 8
CHUNKS = 4
MESH = pl.DeviceIdType.MESH

eps_value = 1e-06

f32 = jnp.float32
bf16 = jnp.bfloat16


def dot(left, right, dims=((1,), (0,))):
    return lax.dot_general(left, right, (dims, ((), ())), preferred_element_type=f32)


def halves(value):
    high = value.astype(bf16)
    return high, (value - high.astype(f32)).astype(bf16)


def product(left, right, dims=((1,), (0,))):
    (lh, ll), (rh, rl) = left, right
    return dot(lh, rh, dims) + (dot(lh, rl, dims) + dot(ll, rh, dims))


def polar_part(coupling, unit):
    parts = halves(coupling)
    a = product(parts, parts, ((1,), (1,)))
    ap = halves(a)
    a2 = product(ap, ap)
    e1 = 0.25 * product(halves(a2), ap) - 0.75 * a2
    e1p = halves(e1)
    sq = product(e1p, e1p)
    e2 = 0.25 * product(halves(sq), e1p) - 0.75 * sq
    off = 0.25 * product(ap, e1p) - 0.5 * (a + e1)
    return unit + (off - 0.5 * (e2 + product(halves(off), halves(e2))))


def kernel(
    plan_ref, factor_ref, out_ref,
    hot, wh, wl, fh, fl, xh, xl, part, from_core, half_sum, from_x, own_sum, from_z, grid_c, ship, land,
    core_send, core_recv, x_send, x_recv, z_send, z_recv, gx_send, gx_recv, gc_send, gc_recv, s_send, s_recv,
):
    pairs = lax.axis_size("pair")
    p, r = lax.axis_index("pair"), lax.axis_index("row")
    core, x, zh = r % 2, (r // 2) % XCHIPS, r // (2 * XCHIPS)
    sibling = (p, r + 1 - 2 * core)
    across = (p, (r + 2 * XCHIPS) % (4 * XCHIPS))
    after, before = ((p + 1) % pairs, r), ((p + pairs - 1) % pairs, r)

    def x_peer(by):
        return (p, zh * (2 * XCHIPS) + ((x + by) % XCHIPS) * 2 + core)

    barrier = pltpu.get_barrier_semaphore()
    for peer in (sibling, x_peer(1), x_peer(2), x_peer(3), across, before):
        pl.semaphore_signal(barrier, inc=1, device_id=peer, device_id_type=MESH)

    rows = out_ref.shape[0]
    step = rows // CHUNKS
    row_ids = lax.broadcasted_iota(jnp.int32, (BLK, BLK), 0)
    col_ids = lax.broadcasted_iota(jnp.int32, (BLK, BLK), 1)
    on_diagonal = row_ids == col_ids

    def remote(src, dst, send, recv, to):
        return pltpu.make_async_remote_copy(
            src_ref=src, dst_ref=dst, send_sem=send, recv_sem=recv, device_id=to, device_id_type=MESH
        )

    started = []

    def reorder(span, high, low):
        moved_h = dot(high, hot[...])
        moved_l = dot(low, hot[...])
        wh[span, :] = moved_h.astype(bf16)
        wl[span, :] = moved_l.astype(bf16)
        moved = moved_h + moved_l
        return jnp.sum(moved * moved, axis=0, keepdims=True)

    def coupling_of(span):
        first = (wh[span, :BLK], wl[span, :BLK])
        second = (wh[span, BLK:], wl[span, BLK:])
        return product(first, second, ((0,), (0,)))

    for rnd in range(ROUNDS):
        order = plan_ref[rnd : rnd + 1, :]
        hot[...] = jnp.where(
            lax.broadcasted_iota(jnp.int32, (WIDTH, WIDTH), 0) == order, 1.0, 0.0
        ).astype(bf16)

        squares = jnp.zeros((1, WIDTH), f32)
        cross = jnp.zeros((BLK, BLK), f32)
        for chunk in range(CHUNKS):
            span = slice(chunk * step, (chunk + 1) * step)
            if rnd == 0:
                high, low = halves(factor_ref[span, :])
            else:
                remote(
                    ship.at[rnd - 1, span, :], land.at[span, :],
                    s_send.at[rnd - 1, chunk], s_recv.at[rnd - 1, chunk], after,
                ).wait_recv()
                sh, sl = halves(land[span, :])
                high = jnp.concatenate([fh[span, :], sh], axis=1)
                low = jnp.concatenate([fl[span, :], sl], axis=1)
            squares += reorder(span, high, low)
            cross += coupling_of(span)

        tile = jnp.concatenate(
            [squares[:, i * LANES : (i + 1) * LANES] for i in range(4)] + [jnp.zeros((4, LANES), f32)], axis=0
        )
        for piece in range(PIECES):
            for side in range(2):
                part[rnd, piece, side * PIECE : (side + 1) * PIECE, :] = cross[
                    piece * PIECE : (piece + 1) * PIECE, side * LANES : (side + 1) * LANES
                ]
            part[rnd, piece, TALL:, :] = tile

        if rnd == 0:
            pl.semaphore_wait(barrier, 6)

        swap = remote(
            part.at[rnd, pl.ds((1 - core) * XCHIPS, XCHIPS)], from_core.at[rnd],
            core_send.at[rnd], core_recv.at[rnd], sibling,
        )
        swap.start()
        started.append(swap)
        swap.wait_recv()
        for other in range(XCHIPS):
            half_sum[rnd, other] = part[rnd, core * XCHIPS + other] + from_core[rnd, other]

        spread = []
        for by in (2, 1, 3):
            copy = remote(
                half_sum.at[rnd, (x + by) % XCHIPS], from_x.at[rnd, by - 1],
                x_send.at[rnd, by - 1], x_recv.at[rnd, by - 1], x_peer(by),
            )
            copy.start()
            spread.append(copy)
        started += spread
        for copy in spread:
            copy.wait_recv()
        own_sum[rnd] = (half_sum[rnd, x] + from_x[rnd, 0]) + (from_x[rnd, 1] + from_x[rnd, 2])

        swap = remote(own_sum.at[rnd], from_z.at[rnd], z_send.at[rnd], z_recv.at[rnd], across)
        swap.start()
        started.append(swap)
        swap.wait_recv()
        total_piece = own_sum[rnd] + from_z[rnd]
        mine = core * XCHIPS + x
        grid_c[rnd, mine] = total_piece[:TALL, :]

        spread = []
        for by in (2, 1, 3):
            copy = remote(
                grid_c.at[rnd, mine], grid_c.at[rnd, mine],
                gx_send.at[rnd, by - 1], gx_recv.at[rnd, by - 1], x_peer(by),
            )
            copy.start()
            spread.append(copy)
        started += spread
        passed = []
        for by in (0, 1, 3, 2):
            slot = core * XCHIPS + (x + XCHIPS - by) % XCHIPS
            if by:
                remote(
                    grid_c.at[rnd, mine], grid_c.at[rnd, slot],
                    gx_send.at[rnd, by - 1], gx_recv.at[rnd, by - 1], x_peer(by),
                ).wait_recv()
            copy = remote(
                grid_c.at[rnd, slot], grid_c.at[rnd, slot], gc_send.at[rnd, by], gc_recv.at[rnd, by], sibling
            )
            copy.start()
            passed.append(copy)
        started += passed
        for copy in passed:
            copy.wait_recv()

        gram_c = jnp.concatenate(
            [
                jnp.concatenate([grid_c[rnd, piece, :PIECE, :], grid_c[rnd, piece, PIECE:, :]], axis=1)
                for piece in range(PIECES)
            ],
            axis=0,
        )
        inverse = 1.0 / jnp.sqrt(total_piece[TALL:, :] + eps_value)
        inv_top = jnp.concatenate([inverse[0:1, :], inverse[1:2, :]], axis=1)
        inv_side = jnp.concatenate([inverse[2:3, :], inverse[3:4, :]], axis=1)
        inv_rows = jnp.sum(jnp.where(on_diagonal, inv_top, 0.0), axis=1, keepdims=True)
        normed = gram_c * inv_rows * inv_side
        total = jnp.sum(jnp.sum(normed * normed, axis=0, keepdims=True), axis=1, keepdims=True)
        coupling = normed * (1.0 / (1.0 + jnp.sqrt(total)))

        unit = jnp.where(on_diagonal, 1.0, 0.0)
        top = polar_part(coupling, unit)
        bottom_parts = halves(polar_part(coupling.T, unit))
        turn = product(halves(coupling), bottom_parts)
        xh[:BLK, :BLK], xl[:BLK, :BLK] = halves(top)
        xh[BLK:, BLK:], xl[BLK:, BLK:] = bottom_parts
        xh[:BLK, BLK:], xl[:BLK, BLK:] = halves(turn)
        xh[BLK:, :BLK], xl[BLK:, :BLK] = halves(-turn.T)

        last = rnd == ROUNDS - 1
        for chunk in range(CHUNKS):
            span = slice(chunk * step, (chunk + 1) * step)
            ship[rnd, span, :] = product((wh[span, :], wl[span, :]), (xh[:, BLK:], xl[:, BLK:]))
            copy = remote(
                ship.at[rnd, span, :], out_ref.at[span, pl.ds(BLK, BLK)] if last else land.at[span, :],
                s_send.at[rnd, chunk], s_recv.at[rnd, chunk], after,
            )
            copy.start()
            started.append(copy)
        for chunk in range(CHUNKS):
            span = slice(chunk * step, (chunk + 1) * step)
            kept = product((wh[span, :], wl[span, :]), (xh[:, :BLK], xl[:, :BLK]))
            if last:
                out_ref[span, :BLK] = kept
            else:
                fh[span, :], fl[span, :] = halves(kept)

    for chunk in range(CHUNKS):
        started[-CHUNKS + chunk].wait_recv()
    for copy in started:
        copy.wait_send()


def shards(factor, plan):
    rows = factor.shape[0]
    dma = pltpu.SemaphoreType.DMA
    return pl.pallas_call(
        kernel,
        out_shape=jax.ShapeDtypeStruct((rows, WIDTH), f32),
        in_specs=[pl.BlockSpec(memory_space=pltpu.VMEM)] * 2,
        out_specs=pl.BlockSpec(memory_space=pltpu.VMEM),
        scratch_shapes=[
            pltpu.VMEM((WIDTH, WIDTH), bf16),
            pltpu.VMEM((rows, WIDTH), bf16),
            pltpu.VMEM((rows, WIDTH), bf16),
            pltpu.VMEM((rows, BLK), bf16),
            pltpu.VMEM((rows, BLK), bf16),
            pltpu.VMEM((WIDTH, WIDTH), bf16),
            pltpu.VMEM((WIDTH, WIDTH), bf16),
            pltpu.VMEM((ROUNDS, PIECES, PACKED, LANES), f32),
            pltpu.VMEM((ROUNDS, XCHIPS, PACKED, LANES), f32),
            pltpu.VMEM((ROUNDS, XCHIPS, PACKED, LANES), f32),
            pltpu.VMEM((ROUNDS, XCHIPS - 1, PACKED, LANES), f32),
            pltpu.VMEM((ROUNDS, PACKED, LANES), f32),
            pltpu.VMEM((ROUNDS, PACKED, LANES), f32),
            pltpu.VMEM((ROUNDS, PIECES, TALL, LANES), f32),
            pltpu.VMEM((ROUNDS, rows, BLK), f32),
            pltpu.VMEM((rows, BLK), f32),
            dma((ROUNDS,)), dma((ROUNDS,)),
            dma((ROUNDS, 3)), dma((ROUNDS, 3)),
            dma((ROUNDS,)), dma((ROUNDS,)),
            dma((ROUNDS, 3)), dma((ROUNDS, 3)),
            dma((ROUNDS, 4)), dma((ROUNDS, 4)),
            dma((ROUNDS, CHUNKS)), dma((ROUNDS, CHUNKS)),
        ],
        compiler_params=pltpu.CompilerParams(collective_id=0, has_side_effects=True),
    )(plan, factor)


def solution(mesh):
    placed = (P("row", "pair"), P())
    return jax.shard_map(
        shards, mesh=mesh, in_specs=placed, out_specs=P("row", "pair"), check_vma=False
    )
```

time: 1140 us -> 96.2 us (0.08)
  waiting for transfers between devices: 813 us -> 0 us
  blocking collectives: 252 us -> 0 us
  Pallas kernels: 0 us -> 93.7 us
  matrix products: 32.9 us -> 0 us
  between operations: 16 us -> 0.01 us
  local copies, waits for them, and re-layouts: 16 us -> 2.26 us
    all_gather x8 -> x0, waiting for transfers between devices: 564 us -> none  [the longest x6 427 us: shards(): piece = lax.all_gather(current, 'row', axis=1, tiled=True)]
    reduce_scatter x2 -> x0, waiting for transfers between devices: 205 us -> none  [shards(): columns = lax.psum_scatter(mixed, 'row', scatter_dimension=1, tiled=True)]
    unnamed x2 -> x0, blocking collectives: 127 us -> none
    psum x2 -> x0, blocking collectives: 125 us -> none  [shards(): total = lax.psum(local_sq, 'row')]
    pallas_call x0 -> x1, Pallas kernels: none -> 93.7 us  [shards(): pl.pallas_call(kernel, out_shape=jax.ShapeDtypeStruct((rows, WIDTH), f32)...]
    ppermute x2 -> x0, waiting for transfers between devices: 43.5 us -> none  [from_behind(): lax.ppermute(value, axis, [(i, (i + by) % devices) for i in range(devices)])]
    dot_general x16 -> x0, matrix products: 32.9 us -> none  [product(): jnp.dot(left, right, precision=lax.Precision.HIGHEST, preferred_element_t...]
  transfers between devices with their start and end apart: 12 -> 0, of which waited for: 12 -> 0; matrix products, arithmetic and copies ran while one was open for 0% -> 0% of each run, Pallas kernels for 0% -> 0%
where the time goes in v1:
time: 96.2 us; the launch traced here: 96 us
  Pallas kernels  93.7 us (97%)
  local copies, waits for them, and re-layouts  2.26 us (2%)
    pallas_call x1, Pallas kernels, shards(): pl.pallas_call(kernel, out_shape=jax.ShapeDtypeStruct((rows, WIDTH), f32)...  93.7 us
    unnamed x1, local copies, waits for them, and re-layouts  2.26 us

profile of v1, /device:TPU:1, one launch (start us, length us, event | category | flops | bytes accessed | tf_op | source)
XLA Modules:
  0.0 96.0 jit_solution(7124729292362674711)
XLA Ops:
  0.0 93.7 %shard_map.28 = f32[512,512]{1,0:T(8,128)} custom-call(s32[2,512]{1,0:T(2,128)} %plan_ref.1, f32[512,512]{1,0:T(8,128)} %factor_ref.1), custom_call_target="tpu_custom_call" | custom-call | tf_op jit(solution)/shard_map/pallas_call | solution.py:244
  93.7 2.3 %copy.4 = f32[512,512]{1,0:T(8,128)} copy(f32[512,512]{1,0:T(8,128)} %shard_map.28) | data formatting | bytes 2097152

commit v2 on v1

--- a/solution.py
+++ b/solution.py
@@ -16,7 +16,8 @@
 PIECE = BLK // PIECES
 TALL = 2 * PIECE
 PACKED = TALL + 8
-CHUNKS = 4
+EDGES = (0, 64, 192, 320, 448, 512)
+SPANS = tuple(slice(low, high) for low, high in zip(EDGES, EDGES[1:]))
 MESH = pl.DeviceIdType.MESH
 
 eps_value = 1e-06
@@ -55,7 +56,7 @@
 def kernel(
     plan_ref, factor_ref, out_ref,
     hot, wh, wl, fh, fl, xh, xl, part, from_core, half_sum, from_x, own_sum, from_z, grid_c, ship, land,
-    core_send, core_recv, x_send, x_recv, z_send, z_recv, gx_send, gx_recv, gc_send, gc_recv, s_send, s_recv,
+    core_send, core_recv, x_send, x_recv, z_send, z_recv, gx_send, gx_recv, gc_send, gc_recv, s_send, s_recv, near_in, far_in,
 ):
     pairs = lax.axis_size("pair")
     p, r = lax.axis_index("pair"), lax.axis_index("row")
@@ -68,11 +69,29 @@
         return (p, zh * (2 * XCHIPS) + ((x + by) % XCHIPS) * 2 + core)
 
     barrier = pltpu.get_barrier_semaphore()
-    for peer in (sibling, x_peer(1), x_peer(2), x_peer(3), across, before):
-        pl.semaphore_signal(barrier, inc=1, device_id=peer, device_id_type=MESH)
-
-    rows = out_ref.shape[0]
-    step = rows // CHUNKS
+
+    def enter(pair, row):
+        pl.semaphore_signal(barrier, inc=1, device_id=(pair, row), device_id_type=MESH)
+
+    for by in (1, 2, 3):
+        enter(p, x_peer(by)[1] - core)
+    enter(across[0], across[1] - core + 1)
+    enter(before[0], before[1] - core + 1)
+
+    @pl.when(core == 1)
+    def _():
+        enter(p, r - 1)
+
+    def pass_on(count, told, teller):
+        @pl.when(core == teller)
+        def _():
+            pl.semaphore_wait(barrier, count)
+            pl.semaphore_signal(told, inc=1, device_id=sibling, device_id_type=MESH)
+
+        @pl.when(core != teller)
+        def _():
+            pl.semaphore_wait(told, 1)
+
     row_ids = lax.broadcasted_iota(jnp.int32, (BLK, BLK), 0)
     col_ids = lax.broadcasted_iota(jnp.int32, (BLK, BLK), 1)
     on_diagonal = row_ids == col_ids
@@ -105,8 +124,7 @@
 
         squares = jnp.zeros((1, WIDTH), f32)
         cross = jnp.zeros((BLK, BLK), f32)
-        for chunk in range(CHUNKS):
-            span = slice(chunk * step, (chunk + 1) * step)
+        for chunk, span in enumerate(SPANS):
             if rnd == 0:
                 high, low = halves(factor_ref[span, :])
             else:
@@ -131,7 +149,7 @@
             part[rnd, piece, TALL:, :] = tile
 
         if rnd == 0:
-            pl.semaphore_wait(barrier, 6)
+            pass_on(7, near_in, 0)
 
         swap = remote(
             part.at[rnd, pl.ds((1 - core) * XCHIPS, XCHIPS)], from_core.at[rnd],
@@ -156,6 +174,8 @@
             copy.wait_recv()
         own_sum[rnd] = (half_sum[rnd, x] + from_x[rnd, 0]) + (from_x[rnd, 1] + from_x[rnd, 2])
 
+        if rnd == 0:
+            pass_on(4, far_in, 1)
         swap = remote(own_sum.at[rnd], from_z.at[rnd], z_send.at[rnd], z_recv.at[rnd], across)
         swap.start()
         started.append(swap)
@@ -206,17 +226,13 @@
         coupling = normed * (1.0 / (1.0 + jnp.sqrt(total)))
 
         unit = jnp.where(on_diagonal, 1.0, 0.0)
-        top = polar_part(coupling, unit)
-        bottom_parts = halves(polar_part(coupling.T, unit))
-        turn = product(halves(coupling), bottom_parts)
-        xh[:BLK, :BLK], xl[:BLK, :BLK] = halves(top)
-        xh[BLK:, BLK:], xl[BLK:, BLK:] = bottom_parts
+        corner = halves(polar_part(coupling.T, unit))
+        turn = product(halves(coupling), corner)
+        xh[BLK:, BLK:], xl[BLK:, BLK:] = corner
         xh[:BLK, BLK:], xl[:BLK, BLK:] = halves(turn)
-        xh[BLK:, :BLK], xl[BLK:, :BLK] = halves(-turn.T)
 
         last = rnd == ROUNDS - 1
-        for chunk in range(CHUNKS):
-            span = slice(chunk * step, (chunk + 1) * step)
+        for chunk, span in enumerate(SPANS):
             ship[rnd, span, :] = product((wh[span, :], wl[span, :]), (xh[:, BLK:], xl[:, BLK:]))
             copy = remote(
                 ship.at[rnd, span, :], out_ref.at[span, pl.ds(BLK, BLK)] if last else land.at[span, :],
@@ -224,16 +240,17 @@
             )
             copy.start()
             started.append(copy)
-        for chunk in range(CHUNKS):
-            span = slice(chunk * step, (chunk + 1) * step)
+        xh[:BLK, :BLK], xl[:BLK, :BLK] = halves(polar_part(coupling, unit))
+        xh[BLK:, :BLK], xl[BLK:, :BLK] = halves(-turn.T)
+        for span in SPANS:
             kept = product((wh[span, :], wl[span, :]), (xh[:, :BLK], xl[:, :BLK]))
             if last:
                 out_ref[span, :BLK] = kept
             else:
                 fh[span, :], fl[span, :] = halves(kept)
 
-    for chunk in range(CHUNKS):
-        started[-CHUNKS + chunk].wait_recv()
+    for copy in started[-len(SPANS):]:
+        copy.wait_recv()
     for copy in started:
         copy.wait_send()
 
@@ -268,9 +285,12 @@
             dma((ROUNDS,)), dma((ROUNDS,)),
             dma((ROUNDS, 3)), dma((ROUNDS, 3)),
             dma((ROUNDS, 4)), dma((ROUNDS, 4)),
-            dma((ROUNDS, CHUNKS)), dma((ROUNDS, CHUNKS)),
+            dma((ROUNDS, len(SPANS))), dma((ROUNDS, len(SPANS))),
+            pltpu.SemaphoreType.REGULAR, pltpu.SemaphoreType.REGULAR,
         ],
-        compiler_params=pltpu.CompilerParams(collective_id=0, has_side_effects=True),
+        compiler_params=pltpu.CompilerParams(
+            collective_id=0, has_side_effects=True, vmem_limit_bytes=20 << 20
+        ),
     )(plan, factor)
 
 

time: 96.2 us -> 87.1 us (0.905)
  Pallas kernels: 93.7 us -> 84.1 us
    pallas_call x1, Pallas kernels: 93.7 us -> 84.1 us  [shards(): pl.pallas_call(kernel, out_shape=jax.ShapeDtypeStruct((rows, WIDTH), f32)...]
    unnamed x1 -> x5, local copies, waits for them, and re-layouts: 2.26 us -> 2.88 us
where the time goes in v2:
time: 87.1 us; the launch traced here: 87 us
  Pallas kernels  84.1 us (97%)
  local copies, waits for them, and re-layouts  2.88 us (3%)
    pallas_call x1, Pallas kernels, shards(): pl.pallas_call(kernel, out_shape=jax.ShapeDtypeStruct((rows, WIDTH), f32)...  84.1 us
    unnamed x5, local copies, waits for them, and re-layouts  2.88 us

profile of v2, /device:TPU:1, one launch (start us, length us, event | category | flops | bytes accessed | tf_op | source)
XLA Modules:
  0.0 87.0 jit_solution(4530009936427075662)
XLA Ops:
  0.0 0.0 copy-start
  0.0 1.2 %copy-done = f32[512,512]{1,0:T(8,128)S(1)} copy-done((f32[512,512]{1,0:T(8,128)S(1)}, f32[512,512]{1,0:T(8,128)}, u32[]{:S(2)}) %copy-start) | copy-done | bytes 1048600
  1.2 0.0 copy-start.1
  1.2 0.7 copy-done.1
  1.9 84.1 %shard_map.28 = f32[512,512]{1,0:T(8,128)S(1)} custom-call(s32[2,512]{1,0:T(2,128)S(1)} %copy-done.1, f32[512,512]{1,0:T(8,128)S(1)} %copy-done), custom_call_target="tpu_custom_call" | custom-call | tf_op jit(solution)/shard_map/pallas_call | solution.py:261
  86.0 1.0 %copy.4 = f32[512,512]{1,0:T(8,128)} copy(f32[512,512]{1,0:T(8,128)S(1)} %shard_map.28) | data formatting | bytes 2097152
Async XLA Ops:
  0.0 1.2 %copy-start = (f32[512,512]{1,0:T(8,128)S(1)}, f32[512,512]{1,0:T(8,128)}, u32[]{:S(2)}) copy-start(f32[512,512]{1,0:T(8,128)} %factor_ref.1) | copy-start | bytes 3145732
  1.2 0.7 copy-start.1

commit v3 on v2

v3 whole, which is shorter than its diff:
```python
import functools

import jax
import jax.numpy as jnp
from jax import lax
from jax.experimental import pallas as pl
from jax.experimental.pallas import tpu as pltpu
from jax.sharding import PartitionSpec as P

BLK = 256
ROUNDS = 2
WIDTH = 2 * BLK
LANES = 128
XCHIPS = 4
PIECES = 8
PIECE = BLK // PIECES
TALL = 2 * PIECE
PACKED = TALL + 8
EARLY = 256
STEP = 64
AHEAD = 3


def spans(low, high, by):
    return tuple(slice(at, min(at + by, high)) for at in range(low, high, by))


FIRST = spans(0, EARLY, STEP)
MESH = pl.DeviceIdType.MESH

eps_value = 1e-06

f32 = jnp.float32
bf16 = jnp.bfloat16


def dot(left, right, dims=((1,), (0,))):
    return lax.dot_general(left, right, (dims, ((), ())), preferred_element_type=f32)


def halves(value):
    high = value.astype(bf16)
    return high, (value - high.astype(f32)).astype(bf16)


def product(left, right, dims=((1,), (0,))):
    (lh, ll), (rh, rl) = left, right
    return dot(lh, rh, dims) + (dot(lh, rl, dims) + dot(ll, rh, dims))


def polar_part(coupling, unit):
    parts = halves(coupling)
    a = product(parts, parts, ((1,), (1,)))
    ap = halves(a)
    a2 = product(ap, ap)
    e1 = 0.25 * product(halves(a2), ap) - 0.75 * a2
    e1p = halves(e1)
    sq = product(e1p, e1p)
    e2 = 0.25 * product(halves(sq), e1p) - 0.75 * sq
    off = 0.25 * product(ap, e1p) - 0.5 * (a + e1)
    return unit + (off - 0.5 * (e2 + product(halves(off), halves(e2))))


def kernel(
    plan_ref, factor_ref, out_ref,
    hot, wh, wl, fh, fl, xh, xl, part, from_core, half_sum, from_x, own_sum, from_z, sum_c, grid_c, ship, land,
    mid, raw, uh, ul, from_before, grid_b,
    core_send, core_recv, x_send, x_recv, z_send, z_recv, gx_send, gx_recv, gc_send, gc_recv, s_send, s_recv,
    r_send, r_recv, b_send, b_recv, bx_send, bx_recv, bc_send, bc_recv, near_in, far_in,
):
    pairs = lax.axis_size("pair")
    p, r = lax.axis_index("pair"), lax.axis_index("row")
    core, x, zh = r % 2, (r // 2) % XCHIPS, r // (2 * XCHIPS)
    sibling = (p, r + 1 - 2 * core)
    across = (p, (r + 2 * XCHIPS) % (4 * XCHIPS))
    after, before = ((p + 1) % pairs, r), ((p + pairs - 1) % pairs, r)
    mine = core * XCHIPS + x

    def x_peer(by):
        return (p, zh * (2 * XCHIPS) + ((x + by) % XCHIPS) * 2 + core)

    barrier = pltpu.get_barrier_semaphore()

    def enter(pair, row):
        pl.semaphore_signal(barrier, inc=1, device_id=(pair, row), device_id_type=MESH)

    for by in (1, 2, 3):
        enter(p, x_peer(by)[1] - core)
    enter(across[0], across[1] - core + 1)
    enter(before[0], before[1] - core + 1)

    @pl.when(core == 1)
    def _():
        enter(p, r - 1)

    def pass_on(count, told, teller):
        @pl.when(core == teller)
        def _():
            pl.semaphore_wait(barrier, count)
            pl.semaphore_signal(told, inc=1, device_id=sibling, device_id_type=MESH)

        @pl.when(core != teller)
        def _():
            pl.semaphore_wait(told, 1)

    row_ids = lax.broadcasted_iota(jnp.int32, (BLK, BLK), 0)
    col_ids = lax.broadcasted_iota(jnp.int32, (BLK, BLK), 1)
    on_diagonal = row_ids == col_ids
    rows = out_ref.shape[0]
    late = spans(EARLY, rows, STEP)

    def remote(src, dst, send, recv, to):
        return pltpu.make_async_remote_copy(
            src_ref=src, dst_ref=dst, send_sem=send, recv_sem=recv, device_id=to, device_id_type=MESH
        )

    started = []

    def go(src, dst, send, recv, to):
        copy = remote(src, dst, send, recv, to)
        copy.start()
        started.append(copy)
        return copy

    def reorder(high, low):
        return dot(high, hot[...]), dot(low, hot[...])

    def gather_start(rnd, src, pieces, sends, recvs):
        for by in (2, 1, 3):
            go(src, pieces.at[rnd, mine], sends.at[rnd, by - 1], recvs.at[rnd, by - 1], x_peer(by))

    def gather_pass(rnd, src, pieces, x_sems, c_sems):
        copies = []
        for by in (0, 1, 3, 2):
            slot = core * XCHIPS + (x + XCHIPS - by) % XCHIPS
            if by:
                remote(
                    src, pieces.at[rnd, slot], x_sems[0].at[rnd, by - 1], x_sems[1].at[rnd, by - 1], x_peer(by)
                ).wait_recv()
            copies.append(
                go(
                    pieces.at[rnd, slot] if by else src, pieces.at[rnd, slot],
                    c_sems[0].at[rnd, by], c_sems[1].at[rnd, by], sibling,
                )
            )
        return copies

    def coupling_of(pieces, tile):
        gram_c = jnp.concatenate(
            [jnp.concatenate([pieces[i, :PIECE, :], pieces[i, PIECE:, :]], axis=1) for i in range(PIECES)], axis=0
        )
        inverse = 1.0 / jnp.sqrt(tile + eps_value)
        inv_top = jnp.concatenate([inverse[0:1, :], inverse[1:2, :]], axis=1)
        inv_side = jnp.concatenate([inverse[2:3, :], inverse[3:4, :]], axis=1)
        inv_rows = jnp.sum(jnp.where(on_diagonal, inv_top, 0.0), axis=1, keepdims=True)
        normed = gram_c * inv_rows * inv_side
        total = jnp.sum(jnp.sum(normed * normed, axis=0, keepdims=True), axis=1, keepdims=True)
        return normed * (1.0 / (1.0 + jnp.sqrt(total)))

    unit = jnp.where(on_diagonal, 1.0, 0.0)

    def second_columns(coupling, high_ref, low_ref):
        corner = halves(polar_part(coupling.T, unit))
        turn = product(halves(coupling), corner)
        high_ref[BLK:, :], low_ref[BLK:, :] = corner
        high_ref[:BLK, :], low_ref[:BLK, :] = halves(turn)
        return turn

    for rnd in range(ROUNDS):
        last = rnd == ROUNDS - 1
        order = plan_ref[rnd : rnd + 1, :]
        hot[...] = jnp.where(
            lax.broadcasted_iota(jnp.int32, (WIDTH, WIDTH), 0) == order, 1.0, 0.0
        ).astype(bf16)

        squares = jnp.zeros((1, WIDTH), f32)
        cross = jnp.zeros((BLK, BLK), f32)
        for spot, span in enumerate(FIRST + late):
            if rnd == 0:
                high, low = halves(factor_ref[span, :])
            elif span.start < EARLY:
                high, low = halves(mid[span, :])
            else:
                chunk = spot - len(FIRST)
                there = slice(span.start - EARLY, span.stop - EARLY)
                remote(
                    ship.at[rnd - 1, there, :], land.at[there, :],
                    s_send.at[rnd - 1, chunk], s_recv.at[rnd - 1, chunk], after,
                ).wait_recv()
                sh, sl = halves(land[there, :])
                high = jnp.concatenate([fh[there, :], sh], axis=1)
                low = jnp.concatenate([fl[there, :], sl], axis=1)
            moved_h, moved_l = reorder(high, low)
            wh[span, :] = moved_h.astype(bf16)
            wl[span, :] = moved_l.astype(bf16)
            moved = moved_h + moved_l
            squares += jnp.sum(moved * moved, axis=0, keepdims=True)
            if span.stop % 256 == 0 or (rnd and span.start >= 384):
                begin = span.start if rnd and span.start >= 384 else span.stop - 256
                if rnd and span.stop == 448:
                    begin = 256
                both = slice(begin, span.stop)
                cross += product(
                    (wh[both, :BLK], wl[both, :BLK]), (wh[both, BLK:], wl[both, BLK:]), ((0,), (0,))
                )

        tile = jnp.concatenate(
            [squares[:, i * LANES : (i + 1) * LANES] for i in range(4)] + [jnp.zeros((4, LANES), f32)], axis=0
        )
        for piece in range(PIECES):
            for side in range(2):
                part[rnd, piece, side * PIECE : (side + 1) * PIECE, :] = cross[
                    piece * PIECE : (piece + 1) * PIECE, side * LANES : (side + 1) * LANES
                ]
            part[rnd, piece, TALL:, :] = tile

        if rnd == 0:
            pass_on(7, near_in, 0)
        go(
            part.at[rnd, pl.ds((1 - core) * XCHIPS, XCHIPS)], from_core.at[rnd],
            core_send.at[rnd], core_recv.at[rnd], sibling,
        ).wait_recv()
        for other in range(XCHIPS):
            half_sum[rnd, other] = part[rnd, core * XCHIPS + other] + from_core[rnd, other]

        spread = [
            go(
                half_sum.at[rnd, (x + by) % XCHIPS], from_x.at[rnd, by - 1],
                x_send.at[rnd, by - 1], x_recv.at[rnd, by - 1], x_peer(by),
            )
            for by in (2, 1, 3)
        ]
        for copy in spread:
            copy.wait_recv()
        own_sum[rnd] = (half_sum[rnd, x] + from_x[rnd, 0]) + (from_x[rnd, 1] + from_x[rnd, 2])

        if rnd == 0:
            pass_on(4, far_in, 1)
        swap = go(own_sum.at[rnd], from_z.at[rnd], z_send.at[rnd], z_recv.at[rnd], across)
        raw_src = mid if rnd else factor_ref
        early = [
            functools.partial(
                go, raw_src.at[span, :], raw.at[rnd, span, :], r_send.at[rnd, chunk], r_recv.at[rnd, chunk], after
            )
            for chunk, span in enumerate(FIRST)
        ]
        arriving = [start() for start in early[:AHEAD]]
        swap.wait_recv()
        sum_c[rnd] = own_sum[rnd] + from_z[rnd]
        grid_c[rnd, mine] = sum_c[rnd, :TALL, :]
        own = sum_c.at[rnd, pl.ds(0, TALL)]
        gather_start(rnd, own, grid_c, gx_send, gx_recv)
        hop = go(sum_c.at[rnd], from_before.at[rnd], b_send.at[rnd], b_recv.at[rnd], after)
        arriving += [start() for start in early[AHEAD:]]
        passed = gather_pass(rnd, own, grid_c, (gx_send, gx_recv), (gc_send, gc_recv))
        hop.wait_recv()
        its = from_before.at[rnd, pl.ds(0, TALL)]
        gather_start(rnd, its, grid_b, bx_send, bx_recv)
        for copy in passed:
            copy.wait_recv()

        coupling = coupling_of(grid_c.at[rnd], sum_c[rnd, TALL:, :])
        turn = second_columns(coupling, xh.at[:, BLK:], xl.at[:, BLK:])
        for chunk, span in enumerate(late):
            there = slice(span.start - EARLY, span.stop - EARLY)
            ship[rnd, there, :] = product((wh[span, :], wl[span, :]), (xh[:, BLK:], xl[:, BLK:]))
            go(
                ship.at[rnd, there, :], out_ref.at[span, pl.ds(BLK, BLK)] if last else land.at[there, :],
                s_send.at[rnd, chunk], s_recv.at[rnd, chunk], after,
            )
        shipped = started[-len(late):]

        grid_b[rnd, mine] = from_before[rnd, :TALL, :]
        passed = gather_pass(rnd, its, grid_b, (bx_send, bx_recv), (bc_send, bc_recv))
        xh[:BLK, :BLK], xl[:BLK, :BLK] = halves(polar_part(coupling, unit))
        xh[BLK:, :BLK], xl[BLK:, :BLK] = halves(-turn.T)
        for span in FIRST + late:
            kept = product((wh[span, :], wl[span, :]), (xh[:, :BLK], xl[:, :BLK]))
            if last:
                out_ref[span, :BLK] = kept
            elif span.start < EARLY:
                mid[span, :BLK] = kept
            else:
                there = slice(span.start - EARLY, span.stop - EARLY)
                fh[there, :], fl[there, :] = halves(kept)
        for copy in passed:
            copy.wait_recv()
        second_columns(coupling_of(grid_b.at[rnd], from_before[rnd, TALL:, :]), uh, ul)
        for copy, span in zip(arriving, FIRST):
            copy.wait_recv()
            moved_h, moved_l = reorder(*halves(raw[rnd, span, :]))
            made = product((moved_h.astype(bf16), moved_l.astype(bf16)), (uh[...], ul[...]))
            if last:
                out_ref[span, BLK:] = made
            else:
                mid[span, BLK:] = made

    for copy in shipped:
        copy.wait_recv()
    for copy in started:
        copy.wait_send()


def shards(factor, plan):
    rows = factor.shape[0]
    rest = rows - EARLY
    chunks = len(spans(EARLY, rows, STEP))
    dma = pltpu.SemaphoreType.DMA

    def both(*shape):
        return [dma(shape), dma(shape)]

    return pl.pallas_call(
        kernel,
        out_shape=jax.ShapeDtypeStruct((rows, WIDTH), f32),
        in_specs=[pl.BlockSpec(memory_space=pltpu.VMEM)] * 2,
        out_specs=pl.BlockSpec(memory_space=pltpu.VMEM),
        scratch_shapes=[
            pltpu.VMEM((WIDTH, WIDTH), bf16),
            pltpu.VMEM((rows, WIDTH), bf16),
            pltpu.VMEM((rows, WIDTH), bf16),
            pltpu.VMEM((rest, BLK), bf16),
            pltpu.VMEM((rest, BLK), bf16),
            pltpu.VMEM((WIDTH, WIDTH), bf16),
            pltpu.VMEM((WIDTH, WIDTH), bf16),
            pltpu.VMEM((ROUNDS, PIECES, PACKED, LANES), f32),
            pltpu.VMEM((ROUNDS, XCHIPS, PACKED, LANES), f32),
            pltpu.VMEM((ROUNDS, XCHIPS, PACKED, LANES), f32),
            pltpu.VMEM((ROUNDS, XCHIPS - 1, PACKED, LANES), f32),
            pltpu.VMEM((ROUNDS, PACKED, LANES), f32),
            pltpu.VMEM((ROUNDS, PACKED, LANES), f32),
            pltpu.VMEM((ROUNDS, PACKED, LANES), f32),
            pltpu.VMEM((ROUNDS, PIECES, TALL, LANES), f32),
            pltpu.VMEM((ROUNDS, rest, BLK), f32),
            pltpu.VMEM((rest, BLK), f32),
            pltpu.VMEM((EARLY, WIDTH), f32),
            pltpu.VMEM((ROUNDS, EARLY, WIDTH), f32),
            pltpu.VMEM((WIDTH, BLK), bf16),
            pltpu.VMEM((WIDTH, BLK), bf16),
            pltpu.VMEM((ROUNDS, PACKED, LANES), f32),
            pltpu.VMEM((ROUNDS, PIECES, TALL, LANES), f32),
            *both(ROUNDS), *both(ROUNDS, 3), *both(ROUNDS), *both(ROUNDS, 3), *both(ROUNDS, 4),
            *both(ROUNDS, chunks), *both(ROUNDS, len(FIRST)), *both(ROUNDS), *both(ROUNDS, 3), *both(ROUNDS, 4),
            pltpu.SemaphoreType.REGULAR, pltpu.SemaphoreType.REGULAR,
        ],
        compiler_params=pltpu.CompilerParams(
            collective_id=0, has_side_effects=True, vmem_limit_bytes=24 << 20
        ),
    )(plan, factor)


def solution(mesh):
    placed = (P("row", "pair"), P())
    return jax.shard_map(
        shards, mesh=mesh, in_specs=placed, out_specs=P("row", "pair"), check_vma=False
    )
```

time: 87.1 us -> 89.2 us (1.024)
  Pallas kernels: 84.1 us -> 86.1 us
    pallas_call x1, Pallas kernels: 84.1 us -> 86.1 us  [shards(): pl.pallas_call(kernel, out_shape=jax.ShapeDtypeStruct((rows, WIDTH), f32)...]
where the time goes in v3:
time: 89.2 us; the launch traced here: 89 us
  Pallas kernels  86.1 us (97%)
  local copies, waits for them, and re-layouts  2.88 us (3%)
    pallas_call x1, Pallas kernels, shards(): pl.pallas_call(kernel, out_shape=jax.ShapeDtypeStruct((rows, WIDTH), f32)...  86.1 us
    unnamed x5, local copies, waits for them, and re-layouts  2.88 us

profile of v3, /device:TPU:1, one launch (start us, length us, event | category | flops | bytes accessed | tf_op | source)
XLA Modules:
  0.0 89.0 jit_solution(11189912335326148860)
XLA Ops:
  0.0 0.0 copy-start
  0.0 1.2 %copy-done = f32[512,512]{1,0:T(8,128)S(1)} copy-done((f32[512,512]{1,0:T(8,128)S(1)}, f32[512,512]{1,0:T(8,128)}, u32[]{:S(2)}) %copy-start) | copy-done | bytes 1048600
  1.2 0.0 copy-start.1
  1.2 0.7 copy-done.1
  1.9 86.1 %shard_map.28 = f32[512,512]{1,0:T(8,128)S(1)} custom-call(s32[2,512]{1,0:T(2,128)S(1)} %copy-done.1, f32[512,512]{1,0:T(8,128)S(1)} %copy-done), custom_call_target="tpu_custom_call" | custom-call | tf_op jit(solution)/shard_map/pallas_call | solution.py:313
  88.0 1.0 %copy.4 = f32[512,512]{1,0:T(8,128)} copy(f32[512,512]{1,0:T(8,128)S(1)} %shard_map.28) | data formatting | bytes 2097152
Async XLA Ops:
  0.0 1.2 %copy-start = (f32[512,512]{1,0:T(8,128)S(1)}, f32[512,512]{1,0:T(8,128)}, u32[]{:S(2)}) copy-start(f32[512,512]{1,0:T(8,128)} %factor_ref.1) | copy-start | bytes 3145732
  1.2 0.7 copy-start.1

commit v4 on v3

--- a/solution.py
+++ b/solution.py
@@ -18,7 +18,8 @@
 PACKED = TALL + 8
 EARLY = 256
 STEP = 64
-AHEAD = 3
+SHIP = 128
+AHEAD = 1
 
 
 def spans(low, high, by):
@@ -45,7 +46,10 @@
 
 def product(left, right, dims=((1,), (0,))):
     (lh, ll), (rh, rl) = left, right
-    return dot(lh, rh, dims) + (dot(lh, rl, dims) + dot(ll, rh, dims))
+    free = 1 - dims[0][0]
+    tall = lh.shape[free]
+    both = dot(jnp.concatenate([lh, ll], axis=free), rh, dims)
+    return both[:tall] + (both[tall:] + dot(lh, rl, dims))
 
 
 def polar_part(coupling, unit):
@@ -55,16 +59,17 @@
     a2 = product(ap, ap)
     e1 = 0.25 * product(halves(a2), ap) - 0.75 * a2
     e1p = halves(e1)
-    sq = product(e1p, e1p)
+    stacked = product([jnp.concatenate(pair, axis=0) for pair in zip(e1p, ap)], e1p)
+    sq = stacked[:BLK]
     e2 = 0.25 * product(halves(sq), e1p) - 0.75 * sq
-    off = 0.25 * product(ap, e1p) - 0.5 * (a + e1)
+    off = 0.25 * stacked[BLK:] - 0.5 * (a + e1)
     return unit + (off - 0.5 * (e2 + product(halves(off), halves(e2))))
 
 
 def kernel(
     plan_ref, factor_ref, out_ref,
     hot, wh, wl, fh, fl, xh, xl, part, from_core, half_sum, from_x, own_sum, from_z, sum_c, grid_c, ship, land,
-    mid, raw, uh, ul, from_before, grid_b,
+    mid, raw, vh, vl, uh, ul, from_before, grid_b,
     core_send, core_recv, x_send, x_recv, z_send, z_recv, gx_send, gx_recv, gc_send, gc_recv, s_send, s_recv,
     r_send, r_recv, b_send, b_recv, bx_send, bx_recv, bc_send, bc_recv, near_in, far_in,
 ):
@@ -107,7 +112,8 @@
     col_ids = lax.broadcasted_iota(jnp.int32, (BLK, BLK), 1)
     on_diagonal = row_ids == col_ids
     rows = out_ref.shape[0]
-    late = spans(EARLY, rows, STEP)
+    whole = slice(0, EARLY)
+    late = spans(EARLY, rows, SHIP)
 
     def remote(src, dst, send, recv, to):
         return pltpu.make_async_remote_copy(
@@ -123,7 +129,8 @@
         return copy
 
     def reorder(high, low):
-        return dot(high, hot[...]), dot(low, hot[...])
+        both = dot(jnp.concatenate([high, low], axis=0), hot[...])
+        return both[: high.shape[0]], both[high.shape[0] :]
 
     def gather_start(rnd, src, pieces, sends, recvs):
         for by in (2, 1, 3):
@@ -175,17 +182,16 @@
 
         squares = jnp.zeros((1, WIDTH), f32)
         cross = jnp.zeros((BLK, BLK), f32)
-        for spot, span in enumerate(FIRST + late):
+        for spot, span in enumerate((whole, slice(EARLY, rows)) if rnd == 0 else (whole,) + late):
             if rnd == 0:
                 high, low = halves(factor_ref[span, :])
-            elif span.start < EARLY:
-                high, low = halves(mid[span, :])
+            elif spot == 0:
+                high, low = halves(mid[...])
             else:
-                chunk = spot - len(FIRST)
                 there = slice(span.start - EARLY, span.stop - EARLY)
                 remote(
                     ship.at[rnd - 1, there, :], land.at[there, :],
-                    s_send.at[rnd - 1, chunk], s_recv.at[rnd - 1, chunk], after,
+                    s_send.at[rnd - 1, spot - 1], s_recv.at[rnd - 1, spot - 1], after,
                 ).wait_recv()
                 sh, sl = halves(land[there, :])
                 high = jnp.concatenate([fh[there, :], sh], axis=1)
@@ -195,14 +201,7 @@
             wl[span, :] = moved_l.astype(bf16)
             moved = moved_h + moved_l
             squares += jnp.sum(moved * moved, axis=0, keepdims=True)
-            if span.stop % 256 == 0 or (rnd and span.start >= 384):
-                begin = span.start if rnd and span.start >= 384 else span.stop - 256
-                if rnd and span.stop == 448:
-                    begin = 256
-                both = slice(begin, span.stop)
-                cross += product(
-                    (wh[both, :BLK], wl[both, :BLK]), (wh[both, BLK:], wl[both, BLK:]), ((0,), (0,))
-                )
+            cross += product((wh[span, :BLK], wl[span, :BLK]), (wh[span, BLK:], wl[span, BLK:]), ((0,), (0,)))
 
         tile = jnp.concatenate(
             [squares[:, i * LANES : (i + 1) * LANES] for i in range(4)] + [jnp.zeros((4, LANES), f32)], axis=0
@@ -261,6 +260,8 @@
 
         coupling = coupling_of(grid_c.at[rnd], sum_c[rnd, TALL:, :])
         turn = second_columns(coupling, xh.at[:, BLK:], xl.at[:, BLK:])
+        xh[:BLK, :BLK], xl[:BLK, :BLK] = halves(polar_part(coupling, unit))
+        xh[BLK:, :BLK], xl[BLK:, :BLK] = halves(-turn.T)
         for chunk, span in enumerate(late):
             there = slice(span.start - EARLY, span.stop - EARLY)
             ship[rnd, there, :] = product((wh[span, :], wl[span, :]), (xh[:, BLK:], xl[:, BLK:]))
@@ -272,28 +273,27 @@
 
         grid_b[rnd, mine] = from_before[rnd, :TALL, :]
         passed = gather_pass(rnd, its, grid_b, (bx_send, bx_recv), (bc_send, bc_recv))
-        xh[:BLK, :BLK], xl[:BLK, :BLK] = halves(polar_part(coupling, unit))
-        xh[BLK:, :BLK], xl[BLK:, :BLK] = halves(-turn.T)
-        for span in FIRST + late:
+        for span in (whole, slice(EARLY, rows)):
             kept = product((wh[span, :], wl[span, :]), (xh[:, :BLK], xl[:, :BLK]))
             if last:
                 out_ref[span, :BLK] = kept
             elif span.start < EARLY:
-                mid[span, :BLK] = kept
+                mid[:, :BLK] = kept
             else:
-                there = slice(span.start - EARLY, span.stop - EARLY)
-                fh[there, :], fl[there, :] = halves(kept)
+                fh[...], fl[...] = halves(kept)
+        for copy in arriving:
+            copy.wait_recv()
+        moved_h, moved_l = reorder(*halves(raw[rnd]))
+        vh[...] = moved_h.astype(bf16)
+        vl[...] = moved_l.astype(bf16)
         for copy in passed:
             copy.wait_recv()
         second_columns(coupling_of(grid_b.at[rnd], from_before[rnd, TALL:, :]), uh, ul)
-        for copy, span in zip(arriving, FIRST):
-            copy.wait_recv()
-            moved_h, moved_l = reorder(*halves(raw[rnd, span, :]))
-            made = product((moved_h.astype(bf16), moved_l.astype(bf16)), (uh[...], ul[...]))
-            if last:
-                out_ref[span, BLK:] = made
-            else:
-                mid[span, BLK:] = made
+        made = product((vh[...], vl[...]), (uh[...], ul[...]))
+        if last:
+            out_ref[whole, BLK:] = made
+        else:
+            mid[:, BLK:] = made
 
     for copy in shipped:
         copy.wait_recv()
@@ -304,7 +304,7 @@
 def shards(factor, plan):
     rows = factor.shape[0]
     rest = rows - EARLY
-    chunks = len(spans(EARLY, rows, STEP))
+    chunks = len(spans(EARLY, rows, SHIP))
     dma = pltpu.SemaphoreType.DMA
 
     def both(*shape):
@@ -335,6 +335,8 @@
             pltpu.VMEM((rest, BLK), f32),
             pltpu.VMEM((EARLY, WIDTH), f32),
             pltpu.VMEM((ROUNDS, EARLY, WIDTH), f32),
+            pltpu.VMEM((EARLY, WIDTH), bf16),
+            pltpu.VMEM((EARLY, WIDTH), bf16),
             pltpu.VMEM((WIDTH, BLK), bf16),
             pltpu.VMEM((WIDTH, BLK), bf16),
             pltpu.VMEM((ROUNDS, PACKED, LANES), f32),

time: 89.2 us -> 79.6 us (0.89)
  Pallas kernels: 86.1 us -> 76.5 us
    pallas_call x1, Pallas kernels: 86.1 us -> 76.5 us  [shards(): pl.pallas_call(kernel, out_shape=jax.ShapeDtypeStruct((rows, WIDTH), f32)...]
where the time goes in v4:
time: 79.6 us; the launch traced here: 79.4 us
  Pallas kernels  76.5 us (96%)
  local copies, waits for them, and re-layouts  2.88 us (4%)
    pallas_call x1, Pallas kernels, shards(): pl.pallas_call(kernel, out_shape=jax.ShapeDtypeStruct((rows, WIDTH), f32)...  76.5 us
    unnamed x5, local copies, waits for them, and re-layouts  2.88 us

profile of v4, /device:TPU:1, one launch (start us, length us, event | category | flops | bytes accessed | tf_op | source)
XLA Modules:
  0.0 79.4 jit_solution(12628090581704797155)
XLA Ops:
  0.0 0.0 copy-start
  0.0 1.2 %copy-done = f32[512,512]{1,0:T(8,128)S(1)} copy-done((f32[512,512]{1,0:T(8,128)S(1)}, f32[512,512]{1,0:T(8,128)}, u32[]{:S(2)}) %copy-start) | copy-done | bytes 1048600
  1.2 0.0 copy-start.1
  1.2 0.7 copy-done.1
  1.9 76.5 %shard_map.28 = f32[512,512]{1,0:T(8,128)S(1)} custom-call(s32[2,512]{1,0:T(2,128)S(1)} %copy-done.1, f32[512,512]{1,0:T(8,128)S(1)} %copy-done), custom_call_target="tpu_custom_call" | custom-call | tf_op jit(solution)/shard_map/pallas_call | solution.py:313
  78.4 1.0 %copy.4 = f32[512,512]{1,0:T(8,128)} copy(f32[512,512]{1,0:T(8,128)S(1)} %shard_map.28) | data formatting | bytes 2097152
Async XLA Ops:
  0.0 1.2 %copy-start = (f32[512,512]{1,0:T(8,128)S(1)}, f32[512,512]{1,0:T(8,128)}, u32[]{:S(2)}) copy-start(f32[512,512]{1,0:T(8,128)} %factor_ref.1) | copy-start | bytes 3145732
  1.2 0.7 copy-start.1

commit v5 on v4

--- a/solution.py
+++ b/solution.py
@@ -16,7 +16,7 @@
 PIECE = BLK // PIECES
 TALL = 2 * PIECE
 PACKED = TALL + 8
-EARLY = 256
+EARLY = 192
 STEP = 64
 SHIP = 128
 AHEAD = 1
@@ -52,18 +52,16 @@
     return both[:tall] + (both[tall:] + dot(lh, rl, dims))
 
 
-def polar_part(coupling, unit):
-    parts = halves(coupling)
-    a = product(parts, parts, ((1,), (1,)))
-    ap = halves(a)
-    a2 = product(ap, ap)
-    e1 = 0.25 * product(halves(a2), ap) - 0.75 * a2
+def polar_factor(b, bp, unit):
+    d1 = 0.25 * product(bp, bp) - 0.75 * b
+    d1p = halves(d1)
+    e1 = product(d1p, bp)
     e1p = halves(e1)
-    stacked = product([jnp.concatenate(pair, axis=0) for pair in zip(e1p, ap)], e1p)
-    sq = stacked[:BLK]
-    e2 = 0.25 * product(halves(sq), e1p) - 0.75 * sq
-    off = 0.25 * stacked[BLK:] - 0.5 * (a + e1)
-    return unit + (off - 0.5 * (e2 + product(halves(off), halves(e2))))
+    psi = 0.25 * e1 - 0.5 * (d1 + unit)
+    t = product(d1p, e1p)
+    step = product(bp, halves(psi))
+    u = 0.25 * product(halves(t), e1p) - 0.75 * t
+    return psi - 0.5 * (u + product(halves(step), halves(u)))
 
 
 def kernel(
@@ -166,12 +164,19 @@
 
     unit = jnp.where(on_diagonal, 1.0, 0.0)
 
-    def second_columns(coupling, high_ref, low_ref):
-        corner = halves(polar_part(coupling.T, unit))
-        turn = product(halves(coupling), corner)
-        high_ref[BLK:, :], low_ref[BLK:, :] = corner
-        high_ref[:BLK, :], low_ref[:BLK, :] = halves(turn)
-        return turn
+    def columns_of(coupling, cp):
+        tp = halves(coupling.T)
+        b = product(tp, tp, ((1,), (1,)))
+        bp = halves(b)
+        phi = halves(polar_factor(b, bp, unit))
+        corner = halves(unit + product(bp, phi))
+        return product(cp, corner), corner, phi, tp
+
+    def turned(rnd, chunk, there):
+        remote(
+            ship.at[rnd, there, :], land.at[rnd, there, :], s_send.at[rnd, chunk], s_recv.at[rnd, chunk], after
+        ).wait_recv()
+        return product(halves(land[rnd, there, :]), (uh[BLK:, :], ul[BLK:, :]))
 
     for rnd in range(ROUNDS):
         last = rnd == ROUNDS - 1
@@ -189,11 +194,7 @@
                 high, low = halves(mid[...])
             else:
                 there = slice(span.start - EARLY, span.stop - EARLY)
-                remote(
-                    ship.at[rnd - 1, there, :], land.at[there, :],
-                    s_send.at[rnd - 1, spot - 1], s_recv.at[rnd - 1, spot - 1], after,
-                ).wait_recv()
-                sh, sl = halves(land[there, :])
+                sh, sl = halves(turned(rnd - 1, spot - 1, there))
                 high = jnp.concatenate([fh[there, :], sh], axis=1)
                 low = jnp.concatenate([fl[there, :], sl], axis=1)
             moved_h, moved_l = reorder(high, low)
@@ -259,22 +260,22 @@
             copy.wait_recv()
 
         coupling = coupling_of(grid_c.at[rnd], sum_c[rnd, TALL:, :])
-        turn = second_columns(coupling, xh.at[:, BLK:], xl.at[:, BLK:])
-        xh[:BLK, :BLK], xl[:BLK, :BLK] = halves(polar_part(coupling, unit))
-        xh[BLK:, :BLK], xl[BLK:, :BLK] = halves(-turn.T)
+        cp = halves(coupling)
         for chunk, span in enumerate(late):
             there = slice(span.start - EARLY, span.stop - EARLY)
-            ship[rnd, there, :] = product((wh[span, :], wl[span, :]), (xh[:, BLK:], xl[:, BLK:]))
+            second = wh[span, BLK:].astype(f32) + wl[span, BLK:].astype(f32)
+            ship[rnd, there, :] = second + product((wh[span, :BLK], wl[span, :BLK]), cp)
             go(
-                ship.at[rnd, there, :], out_ref.at[span, pl.ds(BLK, BLK)] if last else land.at[there, :],
-                s_send.at[rnd, chunk], s_recv.at[rnd, chunk], after,
+                ship.at[rnd, there, :], land.at[rnd, there, :], s_send.at[rnd, chunk], s_recv.at[rnd, chunk], after
             )
-        shipped = started[-len(late):]
+        turn, corner, phi, tp = columns_of(coupling, cp)
+        xh[BLK:, :], xl[BLK:, :] = halves(-turn.T)
+        xh[:BLK, :], xl[:BLK, :] = halves(unit + product(halves(product(cp, phi)), tp))
 
         grid_b[rnd, mine] = from_before[rnd, :TALL, :]
         passed = gather_pass(rnd, its, grid_b, (bx_send, bx_recv), (bc_send, bc_recv))
         for span in (whole, slice(EARLY, rows)):
-            kept = product((wh[span, :], wl[span, :]), (xh[:, :BLK], xl[:, :BLK]))
+            kept = product((wh[span, :], wl[span, :]), (xh[...], xl[...]))
             if last:
                 out_ref[span, :BLK] = kept
             elif span.start < EARLY:
@@ -288,15 +289,18 @@
         vl[...] = moved_l.astype(bf16)
         for copy in passed:
             copy.wait_recv()
-        second_columns(coupling_of(grid_b.at[rnd], from_before[rnd, TALL:, :]), uh, ul)
+        its_coupling = coupling_of(grid_b.at[rnd], from_before[rnd, TALL:, :])
+        its_turn, corner, _, _ = columns_of(its_coupling, halves(its_coupling))
+        uh[BLK:, :], ul[BLK:, :] = corner
+        uh[:BLK, :], ul[:BLK, :] = halves(its_turn)
         made = product((vh[...], vl[...]), (uh[...], ul[...]))
         if last:
             out_ref[whole, BLK:] = made
         else:
             mid[:, BLK:] = made
 
-    for copy in shipped:
-        copy.wait_recv()
+    for chunk, span in enumerate(late):
+        out_ref[span, BLK:] = turned(ROUNDS - 1, chunk, slice(span.start - EARLY, span.stop - EARLY))
     for copy in started:
         copy.wait_send()
 
@@ -321,8 +325,8 @@
             pltpu.VMEM((rows, WIDTH), bf16),
             pltpu.VMEM((rest, BLK), bf16),
             pltpu.VMEM((rest, BLK), bf16),
-            pltpu.VMEM((WIDTH, WIDTH), bf16),
-            pltpu.VMEM((WIDTH, WIDTH), bf16),
+            pltpu.VMEM((WIDTH, BLK), bf16),
+            pltpu.VMEM((WIDTH, BLK), bf16),
             pltpu.VMEM((ROUNDS, PIECES, PACKED, LANES), f32),
             pltpu.VMEM((ROUNDS, XCHIPS, PACKED, LANES), f32),
             pltpu.VMEM((ROUNDS, XCHIPS, PACKED, LANES), f32),
@@ -332,7 +336,7 @@
             pltpu.VMEM((ROUNDS, PACKED, LANES), f32),
             pltpu.VMEM((ROUNDS, PIECES, TALL, LANES), f32),
             pltpu.VMEM((ROUNDS, rest, BLK), f32),
-            pltpu.VMEM((rest, BLK), f32),
+            pltpu.VMEM((ROUNDS, rest, BLK), f32),
             pltpu.VMEM((EARLY, WIDTH), f32),
             pltpu.VMEM((ROUNDS, EARLY, WIDTH), f32),
             pltpu.VMEM((EARLY, WIDTH), bf16),

time: 79.6 us -> 77.2 us (0.970)
  Pallas kernels: 76.5 us -> 74.1 us
    pallas_call x1, Pallas kernels: 76.5 us -> 74.1 us  [shards(): pl.pallas_call(kernel, out_shape=jax.ShapeDtypeStruct((rows, WIDTH), f32)...]
where the time goes in v5:
time: 77.2 us; the launch traced here: 77 us
  Pallas kernels  74.1 us (96%)
  local copies, waits for them, and re-layouts  2.88 us (4%)
    pallas_call x1, Pallas kernels, shards(): pl.pallas_call(kernel, out_shape=jax.ShapeDtypeStruct((rows, WIDTH), f32)...  74.1 us
    unnamed x5, local copies, waits for them, and re-layouts  2.88 us

profile of v5, /device:TPU:1, one launch (start us, length us, event | category | flops | bytes accessed | tf_op | source)
XLA Modules:
  0.0 77.0 jit_solution(8400666865588081111)
XLA Ops:
  0.0 0.0 copy-start
  0.0 1.2 %copy-done = f32[512,512]{1,0:T(8,128)S(1)} copy-done((f32[512,512]{1,0:T(8,128)S(1)}, f32[512,512]{1,0:T(8,128)}, u32[]{:S(2)}) %copy-start) | copy-done | bytes 1048600
  1.2 0.0 copy-start.1
  1.2 0.7 copy-done.1
  1.9 74.1 %shard_map.28 = f32[512,512]{1,0:T(8,128)S(1)} custom-call(s32[2,512]{1,0:T(2,128)S(1)} %copy-done.1, f32[512,512]{1,0:T(8,128)S(1)} %copy-done), custom_call_target="tpu_custom_call" | custom-call | tf_op jit(solution)/shard_map/pallas_call | solution.py:317
  76.1 1.0 %copy.4 = f32[512,512]{1,0:T(8,128)} copy(f32[512,512]{1,0:T(8,128)S(1)} %shard_map.28) | data formatting | bytes 2097152
Async XLA Ops:
  0.0 1.2 %copy-start = (f32[512,512]{1,0:T(8,128)S(1)}, f32[512,512]{1,0:T(8,128)}, u32[]{:S(2)}) copy-start(f32[512,512]{1,0:T(8,128)} %factor_ref.1) | copy-start | bytes 3145732
  1.2 0.7 copy-start.1

commit v6 on v5

--- a/solution.py
+++ b/solution.py
@@ -16,9 +16,9 @@
 PIECE = BLK // PIECES
 TALL = 2 * PIECE
 PACKED = TALL + 8
-EARLY = 192
-STEP = 64
-SHIP = 128
+EARLY = 160
+STEP = 80
+SHIP = 176
 AHEAD = 1
 
 

time: 77.2 us -> 76.8 us (level)
  no operation moved by 1% of the time
where the time goes in v6:
time: 76.8 us; the launch traced here: 76.6 us
  Pallas kernels  73.7 us (96%)
  local copies, waits for them, and re-layouts  2.88 us (4%)
    pallas_call x1, Pallas kernels, shards(): pl.pallas_call(kernel, out_shape=jax.ShapeDtypeStruct((rows, WIDTH), f32)...  73.7 us
    unnamed x5, local copies, waits for them, and re-layouts  2.88 us

profile of v6, /device:TPU:1, one launch (start us, length us, event | category | flops | bytes accessed | tf_op | source)
XLA Modules:
  0.0 76.6 jit_solution(6491377188078797428)
XLA Ops:
  0.0 0.0 copy-start
  0.0 1.2 %copy-done = f32[512,512]{1,0:T(8,128)S(1)} copy-done((f32[512,512]{1,0:T(8,128)S(1)}, f32[512,512]{1,0:T(8,128)}, u32[]{:S(2)}) %copy-start) | copy-done | bytes 1048600
  1.2 0.0 copy-start.1
  1.2 0.7 copy-done.1
  1.9 73.7 %shard_map.28 = f32[512,512]{1,0:T(8,128)S(1)} custom-call(s32[2,512]{1,0:T(2,128)S(1)} %copy-done.1, f32[512,512]{1,0:T(8,128)S(1)} %copy-done), custom_call_target="tpu_custom_call" | custom-call | tf_op jit(solution)/shard_map/pallas_call | solution.py:317
  75.6 1.0 %copy.4 = f32[512,512]{1,0:T(8,128)} copy(f32[512,512]{1,0:T(8,128)S(1)} %shard_map.28) | data formatting | bytes 2097152
Async XLA Ops:
  0.0 1.2 %copy-start = (f32[512,512]{1,0:T(8,128)S(1)}, f32[512,512]{1,0:T(8,128)}, u32[]{:S(2)}) copy-start(f32[512,512]{1,0:T(8,128)} %factor_ref.1) | copy-start | bytes 3145732
  1.2 0.7 copy-start.1

commit v7 on v6

--- a/solution.py
+++ b/solution.py
@@ -17,7 +17,7 @@
 TALL = 2 * PIECE
 PACKED = TALL + 8
 EARLY = 160
-STEP = 80
+STEP = 64
 SHIP = 176
 AHEAD = 1
 

time: 76.8 us -> 77.2 us (level)
  no operation moved by 1% of the time
where the time goes in v7:
time: 77.2 us; the launch traced here: 77 us
  Pallas kernels  74.1 us (96%)
  local copies, waits for them, and re-layouts  2.88 us (4%)
    pallas_call x1, Pallas kernels, shards(): pl.pallas_call(kernel, out_shape=jax.ShapeDtypeStruct((rows, WIDTH), f32)...  74.1 us
    unnamed x5, local copies, waits for them, and re-layouts  2.88 us

profile of v7, /device:TPU:1, one launch (start us, length us, event | category | flops | bytes accessed | tf_op | source)
XLA Modules:
  0.0 77.0 jit_solution(14796205197056026568)
XLA Ops:
  0.0 0.0 copy-start
  0.0 1.2 %copy-done = f32[512,512]{1,0:T(8,128)S(1)} copy-done((f32[512,512]{1,0:T(8,128)S(1)}, f32[512,512]{1,0:T(8,128)}, u32[]{:S(2)}) %copy-start) | copy-done | bytes 1048600
  1.2 0.0 copy-start.1
  1.2 0.7 copy-done.1
  1.9 74.1 %shard_map.28 = f32[512,512]{1,0:T(8,128)S(1)} custom-call(s32[2,512]{1,0:T(2,128)S(1)} %copy-done.1, f32[512,512]{1,0:T(8,128)S(1)} %copy-done), custom_call_target="tpu_custom_call" | custom-call | tf_op jit(solution)/shard_map/pallas_call | solution.py:317
  76.0 1.0 %copy.4 = f32[512,512]{1,0:T(8,128)} copy(f32[512,512]{1,0:T(8,128)S(1)} %shard_map.28) | data formatting | bytes 2097152
Async XLA Ops:
  0.0 1.2 %copy-start = (f32[512,512]{1,0:T(8,128)S(1)}, f32[512,512]{1,0:T(8,128)}, u32[]{:S(2)}) copy-start(f32[512,512]{1,0:T(8,128)} %factor_ref.1) | copy-start | bytes 3145732
  1.2 0.7 copy-start.1
